TPU v7x, 32 devices: a whole 2x2x4 slice. The times are simulated.
32 devices in a mesh: obs: 8 (over z, core), state: 4 (over y, x).
Axes of the slice: x: 2, y: 2, z: 4, core: 2. Of those that a mesh axis runs over, the one named last changes fastest.
Arguments:
- ensemble: bfloat16 [4, 1024, 256], P('state'), may hold values from -16 to 16
- obs_values: float32 [16384], P('obs'), may hold values from -72 to 72
- obs_error: float32 [16384], P('obs'), may hold values from 6 to 24
- h_blocks: bfloat16 [8, 4, 64, 128, 128], P('obs', 'state'), may hold values from -0.125 to 0.125
- block_rows: int32 [8, 4, 64], P('obs', 'state'), may hold values from 0 to 15
- block_cols: int32 [8, 4, 64], P('obs', 'state'), may hold values from 0 to 7
- block_count: int32 [8, 4], P('obs', 'state'), may hold values from 32 to 64, as said below
Outputs:
- analysis: bfloat16 [4, 1024, 256], P('state', 'obs')
Inputs may be any that keep to these rules, and one draw needn't show every extreme that they name: `block_count`: some device has exactly 64 live slots in every draw.
All inputs are finite; a program needn't handle non-finite values.
Results may differ from a plain program's by a relative error of at most 0.009.
Values sent between devices are 32-bit elements; how exact they have to be, the bound alone decides.
A program may use at most 64 MiB of HBM per device.

v0:
```python
import math

import jax
import jax.numpy as jnp
from jax import lax
from jax.sharding import PartitionSpec as P

K = 256
BS = 128
M_DEV = 2048
BLK_DEV = 64


def on_device(ensemble, obs_values, obs_error, h_blocks, block_rows, block_cols, block_count):
    members = ensemble[0]
    slab_rows = members.shape[0]
    state_blocks = slab_rows // BS
    obs_blocks = M_DEV // BS
    member_blocks = members.reshape(state_blocks, BS, K)
    group_size = math.gcd(BLK_DEV, 32)
    group_count = BLK_DEV // group_size
    all_blocks = h_blocks[0, 0]
    all_cols = block_cols[0, 0]
    all_rows = block_rows[0, 0]
    live_count = block_count[0, 0]
    block_ids = jnp.arange(obs_blocks, dtype=jnp.int32)

    def add_group(group_index, carry):
        start = (group_index * group_size).astype(jnp.int32)
        blocks = lax.dynamic_slice_in_dim(all_blocks, start, group_size, 0)
        cols = lax.dynamic_slice_in_dim(all_cols, start, group_size, 0)
        rows = lax.dynamic_slice_in_dim(all_rows, start, group_size, 0)
        live_mask = start + jnp.arange(group_size, dtype=jnp.int32) < live_count
        picked = member_blocks[cols]
        products = jnp.einsum("bij,bjk->bik", blocks, picked, preferred_element_type=jnp.float32)
        upper_part = products.astype(jnp.bfloat16)
        lower_part = (products - upper_part.astype(jnp.float32)).astype(jnp.bfloat16)
        onehot = ((rows[None, :] == block_ids[:, None]) & live_mask[None, :]).astype(jnp.bfloat16)
        carry = carry + jnp.einsum(
            "mb,bik->mik", onehot, upper_part, preferred_element_type=jnp.float32
        )
        carry = carry + jnp.einsum(
            "mb,bik->mik", onehot, lower_part, preferred_element_type=jnp.float32
        )
        return carry

    accumulated = lax.fori_loop(
        0, group_count, add_group, jnp.zeros((obs_blocks, BS, K), jnp.float32)
    )
    slab_term = accumulated.reshape(M_DEV, K)
    state_devices = lax.axis_size("state")
    rows_share = M_DEV // state_devices
    row_offset = lax.axis_index("state") * rows_share
    own_rows = lax.psum_scatter(slab_term, "state", scatter_dimension=0, tiled=True)
    own_values = lax.dynamic_slice_in_dim(obs_values, row_offset, rows_share, 0)
    own_errors = lax.dynamic_slice_in_dim(obs_error, row_offset, rows_share, 0)
    obs_mean = jnp.mean(own_rows, axis=1)
    whitened = (own_rows - obs_mean[:, None]) / own_errors[:, None]
    innovation = (own_values - obs_mean) / own_errors
    gram_part = lax.dot_general(
        whitened, whitened, (((0,), (0,)), ((), ())), precision=lax.Precision.HIGHEST
    )
    projected_part = jnp.dot(innovation, whitened, precision=lax.Precision.HIGHEST)
    identity = jnp.eye(K, dtype=jnp.float32)
    gram_sum, projected_innovation = lax.psum((gram_part, projected_part), ("obs", "state"))
    lower_factor = jnp.linalg.cholesky(gram_sum + (K - 1) * identity)
    halfway = lax.linalg.triangular_solve(
        lower_factor, projected_innovation[:, None], left_side=True, lower=True
    )
    mean_weight = lax.linalg.triangular_solve(
        lower_factor, halfway, left_side=True, lower=True, transpose_a=True
    )
    root_inverse = lax.linalg.triangular_solve(
        lower_factor, identity, left_side=True, lower=True, transpose_a=True
    )
    transform = (math.sqrt(K - 1) * root_inverse + mean_weight).astype(jnp.bfloat16)
    piece_rows = slab_rows // lax.axis_size("obs")
    own_piece = lax.dynamic_slice_in_dim(
        members, lax.axis_index("obs") * piece_rows, piece_rows, 0
    ).astype(jnp.float32)
    state_mean = jnp.mean(own_piece, axis=1)
    anomalies = (own_piece - state_mean[:, None]).astype(jnp.bfloat16)
    analysis = state_mean[:, None] + jnp.dot(
        anomalies, transform, preferred_element_type=jnp.float32
    )
    return analysis.astype(jnp.bfloat16)[None]


def solution(mesh):
    placed = (
        P("state", None, None),
        P("obs"),
        P("obs"),
        P("obs", "state", None, None, None),
        P("obs", "state", None),
        P("obs", "state", None),
        P("obs", "state"),
    )
    return jax.shard_map(
        on_device, mesh=mesh, in_specs=placed, out_specs=P("state", "obs", None), check_vma=False
    )
```

profile of v0, /device:TPU:0, one launch (start us, length us, event | category | flops | bytes accessed | tf_op | source)
XLA Modules:
  0.0 278.9 jit_solution(10647405630408804250)
XLA Ops:
  6.5 0.0 reduce-scatter.2.cloned.1.call-start
  6.5 24.7 %while.16 = (s32[]{:T(128)}, f32[16,128,256]{2,0,1:T(8,128)}, s32[64]{0:T(128)}, s32[]{:T(128)}, bf16[64,128,128]{2,1,0:T(8,128)(2,1)}, /*index=5*/s32[64]{0:T(1...) while((s32[]{:T(128)}, f32[16,128,256]{2,0,1:T(8,128)}, ...), condition=%wide.region_2.0_spmd.clone, body=%wide.region_1.0_spmd.clone.sunk | while | flops 341314720 | bytes 24123700 | solution.py:47
  6.5 0.7 compare_select_fusion.2
  7.3 1.7 gather_fusion
  9.0 0.0 copy-start.1
  9.0 3.2 %subtract_convert_fusion.2 = (bf16[32,128,256]{2,1,0:T(8,128)(2,1)S(1)}, bf16[32,128,256]{2,1,0:T(8,128)(2,1)}) fusion(bf16[32,128,256]{2,1,0:T(8,128)(2,1)S(1)} %gather_fusion, bf16[64,128,128]{2,1,0:T(8,128)(2,1)} %get-tuple-element.322, s32[]{:T(128)S(6)} %select_n.37), kind=kOutput, calls=%fused_computation.4.clone.1 | convolution fusion | flops 272629760 | bytes 7340036 | tf_op jit(solution)/shard_map/while/body/eval_jaxpr/bij,bjk->bik/dot_general | solution.py:35
  12.2 0.0 copy-done.1
  12.2 0.1 dynamic_slice.54
  12.3 0.7 add_compare_fusion.2
  13.0 1.3 fusion.80
  14.2 4.3 %fusion.81 = f32[16,128,256]{2,0,1:T(8,128)} fusion(f32[16,128,256]{2,0,1:T(8,128)S(1)} %fusion.80, f32[16,128,256]{2,0,1:T(8,128)} %get-tuple-element.308, bf16[32,128,256]{2,1,0:T(8,128)(2,1)} %get-tuple-element.295, pred[]{:T(512)S(6)} %compare.30, s32[32]{0:T(128)S(1)} %dynamic_slice.54, pred[32]{0:T(512)(128)(4,1)S(1)} %add_compare_fusion.2), kind=kOutput, calls=%fused_computation.10.clone.1 | convolution fusion | flops 35128320 | bytes 8388769 | tf_op jit(solution)/shard_map/while/body/eval_jaxpr/mb,bik->mik/dot_general | solution.py:39
  18.6 0.7 compare_select_fusion.2
  19.3 1.7 gather_fusion
  21.0 0.0 copy-start.1
  21.0 3.2 %subtract_convert_fusion.2 = (bf16[32,128,256]{2,1,0:T(8,128)(2,1)S(1)}, bf16[32,128,256]{2,1,0:T(8,128)(2,1)}) fusion(bf16[32,128,256]{2,1,0:T(8,128)(2,1)S(1)} %gather_fusion, bf16[64,128,128]{2,1,0:T(8,128)(2,1)} %get-tuple-element.322, s32[]{:T(128)S(6)} %select_n.37), kind=kOutput, calls=%fused_computation.4.clone.1 | convolution fusion | flops 272629760 | bytes 7340036 | tf_op jit(solution)/shard_map/while/body/eval_jaxpr/bij,bjk->bik/dot_general | solution.py:35
  24.3 0.0 copy-done.1
  24.3 0.1 dynamic_slice.54
  24.3 0.7 add_compare_fusion.2
  25.0 1.3 fusion.80
  26.3 5.0 %fusion.81 = f32[16,128,256]{2,0,1:T(8,128)} fusion(f32[16,128,256]{2,0,1:T(8,128)S(1)} %fusion.80, f32[16,128,256]{2,0,1:T(8,128)} %get-tuple-element.308, bf16[32,128,256]{2,1,0:T(8,128)(2,1)} %get-tuple-element.295, pred[]{:T(512)S(6)} %compare.30, s32[32]{0:T(128)S(1)} %dynamic_slice.54, pred[32]{0:T(512)(128)(4,1)S(1)} %add_compare_fusion.2), kind=kOutput, calls=%fused_computation.10.clone.1 | convolution fusion | flops 35128320 | bytes 8388769 | tf_op jit(solution)/shard_map/while/body/eval_jaxpr/mb,bik->mik/dot_general | solution.py:39
  31.2 4.1 %copy.18 = f32[16,128,256]{2,1,0:T(8,128)} copy(f32[16,128,256]{2,0,1:T(8,128)} %get-tuple-element.144) | data formatting | bytes 4194304 | tf_op jit(solution)/shard_map/while | solution.py:47
  35.3 0.0 reduce-scatter.2.cloned.1.call-update
  35.4 0.0 all-reduce.3.cloned.1.call-start
  35.4 0.9 convert_reduce_fusion
  36.4 37.0 %reduce-scatter.2.cloned.1.call-done = f32[512,256]{1,0:T(8,128)} async-done(((f32[2048,256]{1,0:T(8,128)}), f32[512,256]{1,0:T(8,128)}) %reduce-scatter.2.cloned.1.call-update) | async-done | bytes 524304 | tf_op jit(solution)/shard_map/reduce_scatter | solution.py:54
  73.4 1.3 reduce_sum.19
  74.7 0.8 subtract_divide_fusion.1
  75.5 3.2 %fusion.54 = f32[256,256]{0,1:T(8,128)} fusion(f32[512,256]{1,0:T(8,128)} %reduce-scatter.2.cloned.1.call-done, f32[512]{0:T(512)S(1)} %get-tuple-element.216, f32[512]{0:T(512)S(1)} %get-tuple-element.217), kind=kOutput, calls=%fused_computation.89 | convolution fusion | flops 402915328 | bytes 790528 | tf_op jit(solution)/shard_map/dot_general | solution.py:60
  78.7 0.0 all-reduce.3.cloned.1.call-update
  78.7 0.0 copy-done
  78.7 0.4 fusion.53
  79.2 39.5 %psum.15 = f32[256]{0:T(256)S(1)} all-reduce(f32[256]{0:T(256)S(1)} %bitcast.108), channel_id=1, replica_groups=mesh['obs'=8,'state'=4] {'obs','state'}, use_global_device_ids=true, to_apply=%region_10.11 | all-reduce | flops 256 | bytes 2048 | tf_op jit(solution)/shard_map/psum | solution.py:65
  118.6 87.0 %all-reduce.3.cloned.1.call-done = f32[256,256]{0,1:T(8,128)} async-done(((f32[256,256]{0,1:T(8,128)}), f32[256,256]{0,1:T(8,128)}) %all-reduce.3.cloned.1.call-update) | async-done | bytes 262160 | tf_op jit(solution)/shard_map/psum | solution.py:65
  205.6 1.0 select_add_fusion.1
  206.6 0.1 copy.20
  206.7 1.0 fusion.28
  207.7 11.7 %cholesky.49 = f32[128,128]{1,0:T(8,128)S(1)} custom-call(f32[128,128]{1,0:T(8,128)S(1)} %cholesky.115), custom_call_target="Cholesky" | custom-call | tf_op jit(solution)/shard_map/jit(cholesky)/cholesky | solution.py:66
  219.5 9.8 %custom-call.18 = f32[1,128,128]{1,2,0:T(8,128)S(1)} custom-call(f32[1,128,128]{2,1,0:T(8,128)S(1)} %get-tuple-element.214), custom_call_target="InvertDiagBlocksLowerTriangular" | custom-call | tf_op jit(solution)/shard_map/jit(cholesky)/cholesky | solution.py:66
  229.3 0.2 fusion.37
  229.5 0.3 convolution_subtract_fusion.1
  229.8 11.7 %cholesky.103 = f32[128,128]{1,0:T(8,128)S(1)} custom-call(f32[128,128]{1,0:T(8,128)S(1)} %convolution_subtract_fusion.1), custom_call_target="Cholesky" | custom-call | tf_op jit(solution)/shard_map/jit(cholesky)/cholesky | solution.py:66
  241.5 0.1 copy.23
  241.6 0.1 copy.22
  241.7 0.1 copy.21
  241.9 0.7 compare_reduce_fusion
  243.9 0.1 triangular_solve.94
  244.0 4.3 %while.15 = (s32[]{:T(128)}, f32[256,256]{0,1:T(8,128)S(1)}, s32[2,2]{1,0:T(2,128)S(1)}, f32[2,128,128]{2,1,0:T(8,128)S(1)}, s32[]{:T(128)}) while((s32[]{:T(128)}, f32[256,256]{0,1:T(8,128)S(1)}, s32[2,2]{1,0:T(2,128)S(1)}, f32[2,128,128]{2,1,0:T(8,128)S(1)}, s32[]{:T(128)}) %tuple.58), condition=%wide.while_cond, body=%wide.while_body.sunk | while | flops 2 | bytes 393321 | solution.py:73
  244.0 0.7 fusion.74
  244.6 1.3 dynamic-slice.8
  246.0 0.1 copy.36
  246.1 0.7 fusion.74
  246.8 1.3 dynamic-slice.8
  248.1 0.1 copy.36
  248.3 19.9 %custom-call.19 = f32[2,128,128]{1,2,0:T(8,128)S(1)} custom-call(f32[2,128,128]{2,1,0:T(8,128)S(1)} %get-tuple-element.152), custom_call_target="InvertDiagBlocksLowerTriangular" | custom-call | tf_op jit(solution)/shard_map/triangular_solve | solution.py:73
  268.2 0.2 fusion.41
  268.3 0.2 fusion.25
  268.5 0.2 convolution_bitcast_fusion.3
  268.7 0.2 convolution_bitcast_fusion.2
  268.9 0.2 fusion.23
  269.1 0.2 convolution_bitcast_fusion
  269.3 0.3 fusion.34
  269.6 0.4 convolution_subtract_fusion
  270.0 0.3 fusion.42
  270.3 1.7 fusion.21
  (20 shorter events, 0.2 us)
Async XLA Ops:
  6.5 66.9 %reduce-scatter.2.cloned.1.call-start = ((), (), s32[]{:S(2)}) async-start(), calls=%async_computation.1 | async-start | bytes 2621440 | tf_op jit(solution)/shard_map/reduce_scatter | solution.py:54
  9.0 3.2 %copy-start.1 = (s32[64]{0:T(128)S(1)}, s32[64]{0:T(128)}, u32[]{:S(2)}) copy-start(s32[64]{0:T(128)} %get-tuple-element.320) | copy-start | bytes 772 | tf_op jit(solution)/shard_map/while
  21.0 3.2 %copy-start.1 = (s32[64]{0:T(128)S(1)}, s32[64]{0:T(128)}, u32[]{:S(2)}) copy-start(s32[64]{0:T(128)} %get-tuple-element.320) | copy-start | bytes 772 | tf_op jit(solution)/shard_map/while
  35.4 170.3 %all-reduce.3.cloned.1.call-start = ((), (), s32[]{:S(2)}) async-start(), calls=%async_computation.2 | async-start | bytes 524288 | tf_op jit(solution)/shard_map/psum | solution.py:65
  73.4 5.3 %copy-start = (f32[512,256]{1,0:T(8,128)S(1)}, f32[512,256]{1,0:T(8,128)}, u32[]{:S(2)}) copy-start(f32[512,256]{1,0:T(8,128)} %reduce-scatter.2.cloned.1.call-done) | copy-start | bytes 1572868
Sparse Core Ops, SparseCore 0:
  35.5 37.9 reduce-scatter.1
  78.9 126.6 all-reduce.2
where the time goes:
time: 280 us; the launch traced here: 279 us
  waiting for transfers between devices  124 us (44%)
  other arithmetic  61.7 us (22%)
  blocking collectives  39.5 us (14%)
  matrix products  26.2 us (9%)
  between operations  14.9 us (5%)
  local copies, waits for them, and re-layouts  12.4 us (4%)
    psum x1, waiting for transfers between devices, on_device(): lax.psum((gram_part, projected_part), ('obs', 'state'))  87 us
    psum x1, blocking collectives, on_device(): lax.psum((gram_part, projected_part), ('obs', 'state'))  39.5 us
    reduce_scatter x1, waiting for transfers between devices, on_device(): lax.psum_scatter(slab_term, 'state', scatter_dimension=0, tiled=True)  37 us
    another operation x6, other arithmetic, on_device(): lower_factor = jnp.linalg.cholesky(gram_sum + (K - 1) * identity)  34 us
    another operation x3, other arithmetic, on_device(): lax.linalg.triangular_solve(lower_factor, identity, left_side=True, lower...  19.9 us
    dot_general x2, matrix products, add_group(): jnp.einsum('mb,bik->mik', onehot, upper_part, preferred_element_type=jnp....  9.29 us
    dot_general x2, matrix products, add_group(): jnp.einsum('bij,bjk->bik', blocks, picked, preferred_element_type=jnp.flo...  6.45 us
  transfers between devices with their start and end apart: 2, of which 2 were waited for; matrix products, arithmetic and copies ran while one was open for 1% of the time, Pallas kernels for 0%

commit v1 on v0

v1 whole, which is shorter than its diff:
```python
import functools
import math

import jax
import jax.numpy as jnp
from jax import lax
from jax.experimental import pallas as pl
from jax.experimental.pallas import tpu as pltpu
from jax.sharding import PartitionSpec as P

LANES = 128
MESH = pl.DeviceIdType.MESH
VMEM = pl.BlockSpec(memory_space=pltpu.VMEM)
SMEM = pl.BlockSpec(memory_space=pltpu.SMEM)
ANY = pl.BlockSpec(memory_space=pl.ANY)
HIGHEST = lax.Precision.HIGHEST


def project_kernel(groups, rows_ref, cols_ref, count_ref, members_hbm, blocks_hbm, out_ref, members, blocks, sems):
    slots = blocks.shape[0]
    per = slots // groups
    spare = out_ref.shape[1] - 1
    load_members = pltpu.make_async_copy(members_hbm, members, sems.at[groups])
    load_members.start()
    loads = []
    for g in range(groups):
        part = pl.ds(g * per, per)
        loads.append(pltpu.make_async_copy(blocks_hbm.at[part], blocks.at[part], sems.at[g]))
        loads[-1].start()
    out_ref[...] = jnp.zeros_like(out_ref)
    live = count_ref[0, 0]
    load_members.wait()
    for g in range(groups):
        loads[g].wait()

        def add_some(step, carry, g=g):
            base = g * per + step * 4
            products = []
            for k in range(4):
                products.append(
                    jnp.dot(blocks[base + k], members[cols_ref[0, base + k]], preferred_element_type=jnp.float32)
                )
            for k in range(4):
                slot = base + k
                row = jnp.where(slot < live, rows_ref[0, slot], spare)
                out_ref[0, row] += products[k][:, :LANES]
                out_ref[1, row] += products[k][:, LANES:]
            return carry

        lax.fori_loop(0, per // 4, add_some, 0)


def project(members, blocks, rows, cols, count, obs_blocks):
    slots, size, unused = blocks.shape
    width = members.shape[-1]
    groups = 4
    return pl.pallas_call(
        functools.partial(project_kernel, groups),
        out_shape=jax.ShapeDtypeStruct((2, obs_blocks + 1, size, width // 2), jnp.float32),
        in_specs=[SMEM, SMEM, SMEM, ANY, ANY],
        out_specs=VMEM,
        scratch_shapes=[
            pltpu.VMEM(members.shape, members.dtype),
            pltpu.VMEM(blocks.shape, blocks.dtype),
            pltpu.SemaphoreType.DMA((groups + 1,)),
        ],
        name="project",
    )(rows, cols, count, members, blocks)


def stage_plan(bits, order):
    plan = []
    for at, bit in enumerate(order):
        later = order[at + 1:]
        kept = [0]
        for other in later:
            kept = kept + [rel | (1 << other) for rel in kept]
        kept = sorted(kept, key=lambda rel: [-((rel >> other) & 1) for other in later])
        plan.append((bit, kept))
    return plan


def columns_of(row):
    return jnp.transpose(jnp.broadcast_to(row, (LANES, LANES)))


def combine_kernel(n_obs, n_state, terms, values_ref, errors_ref, out_ref, got0, got1, errs, innov, white, gram, part_in, mine, z_in, full, send, recv, send_b, recv_b):
    state = lax.axis_index("state")
    obs = lax.axis_index("obs")
    core = obs % 2
    z = obs // 2
    n_z = n_obs // 2
    bits = int(math.log2(n_state))
    group = n_state * 2
    share = white.shape[0]
    members = white.shape[1]
    per = share // LANES

    def flipped(rel):
        total = 0
        for bit in range(bits):
            own = (state // (1 << bit)) % 2
            total = total + (1 << bit) * ((own + ((rel >> bit) & 1)) % 2)
        return total

    peers = []
    for shift in range(1, group):
        index = (state * 2 + core + shift) % group
        peers.append((z * 2 + index % 2, index // 2))
    z_peers = [(((z + shift) % n_z) * 2 + core, state) for shift in range(1, n_z)]

    barrier = pltpu.get_barrier_semaphore()
    for peer in peers + z_peers:
        pl.semaphore_signal(barrier, inc=1, device_id=peer, device_id_type=MESH)
    pl.semaphore_wait(barrier, len(peers) + len(z_peers))

    def piece(half, index):
        return terms.at[half, pl.ds(index * per, per)]

    got = (got0, got1)
    plans = (stage_plan(bits, list(range(bits))), stage_plan(bits, list(range(bits))[::-1]))
    slot_of = []
    for plan in plans:
        slots = {}
        for at, (bit, kept) in enumerate(plan):
            for rel in kept:
                slots[at, rel] = len(slots)
        slot_of.append(slots)
    copies = {}

    def launch(half, at, rel):
        bit = plans[half][at][0]
        sent_rel = rel | (1 << bit)
        if at == 0:
            source = piece(half, flipped(sent_rel))
        else:
            source = got[half].at[slot_of[half][at - 1, sent_rel]]
        slot = slot_of[half][at, rel]
        copy = pltpu.make_async_remote_copy(
            src_ref=source,
            dst_ref=got[half].at[slot],
            send_sem=send.at[half, slot],
            recv_sem=recv.at[half, slot],
            device_id=(obs, flipped(1 << bit)),
            device_id_type=MESH,
        )
        copy.start()
        copies[half, at, rel] = copy

    for index in range(len(plans[0][0][1])):
        for half in range(2):
            launch(half, 0, plans[half][0][1][index])
    for k in range(per):
        at_rows = pl.ds(k * LANES, LANES)
        errs[at_rows] = columns_of(errors_ref[pl.ds(state * per + k, 1), :])
        innov[at_rows] = columns_of(values_ref[pl.ds(state * per + k, 1), :])
    for at in range(bits):
        for index in range(len(plans[0][at][1])):
            for half in range(2):
                rel = plans[half][at][1][index]
                copies[half, at, rel].wait_recv()
                slot = slot_of[half][at, rel]
                if at == 0:
                    got[half][slot] += terms[half, pl.ds(flipped(rel) * per, per)]
                else:
                    got[half][slot] += got[half][slot_of[half][at - 1, rel]]
                if at + 1 < bits and (rel >> plans[half][at + 1][0]) & 1:
                    launch(half, at + 1, rel ^ (1 << plans[half][at + 1][0]))
    last = [slot_of[half][bits - 1, 0] for half in range(2)]
    low, high = [got[half][last[half]].reshape(share, LANES) for half in range(2)]
    mean = (jnp.sum(low, axis=1, keepdims=True) + jnp.sum(high, axis=1, keepdims=True)) / members
    white[:, :LANES] = (low - mean) / errs[...]
    white[:, LANES:] = (high - mean) / errs[...]
    weight = (innov[...] - mean) / errs[...]
    whole = white[...]
    gram[...] = lax.dot_general(
        whole, whole, (((0,), (0,)), ((), ())), precision=HIGHEST, preferred_element_type=jnp.float32
    )
    gram[0:1, LANES:] = jnp.sum(whole[:, :LANES] * weight, axis=0, keepdims=True)
    gram[1:2, LANES:] = jnp.sum(whole[:, LANES:] * weight, axis=0, keepdims=True)

    own = state * 2 + core
    rows = members // group

    def rows_of(index):
        return pl.ds(index * rows, rows)

    def send_to(source, target, at, peer):
        copy = pltpu.make_async_remote_copy(
            src_ref=source,
            dst_ref=target,
            send_sem=send_b.at[at],
            recv_sem=recv_b.at[at],
            device_id=peer,
            device_id_type=MESH,
        )
        copy.start()
        return copy

    first = []
    for k, peer in enumerate(peers):
        index = (own + k + 1) % group
        first.append(send_to(gram.at[rows_of(index)], part_in.at[k], k, peer))
    total = gram[rows_of(own), :]
    for k, copy in enumerate(first):
        copy.wait_recv()
        total = total + part_in[k]
    mine[...] = total
    second = []
    for k, peer in enumerate(z_peers):
        second.append(send_to(mine, z_in.at[k], group - 1 + k, peer))
    for k, copy in enumerate(second):
        copy.wait_recv()
        total = total + z_in[k]
    full[rows_of(own), :] = total
    third = []
    for k, peer in enumerate(peers):
        third.append(send_to(full.at[rows_of(own)], full.at[rows_of(own)], group - 1 + n_z - 1 + k, peer))
    for copy in third:
        copy.wait_recv()
    out_ref[...] = full[...]
    for copy in list(copies.values()) + first + second + third:
        copy.wait_send()


def combine(terms, values, errors, n_obs, n_state, obs_blocks):
    size = terms.shape[2]
    members = 2 * terms.shape[3]
    per = obs_blocks // n_state
    group = 2 * n_state
    n_z = n_obs // 2
    count = n_state - 1
    others = 2 * (group - 1) + n_z - 1
    return pl.pallas_call(
        functools.partial(combine_kernel, n_obs, n_state),
        out_shape=jax.ShapeDtypeStruct((members, members), jnp.float32),
        in_specs=[VMEM] * 3,
        out_specs=VMEM,
        scratch_shapes=[
            pltpu.VMEM((count, per, size, members // 2), jnp.float32),
            pltpu.VMEM((count, per, size, members // 2), jnp.float32),
            pltpu.VMEM((per * size, LANES), jnp.float32),
            pltpu.VMEM((per * size, LANES), jnp.float32),
            pltpu.VMEM((per * size, members), jnp.float32),
            pltpu.VMEM((members, members), jnp.float32),
            pltpu.VMEM((group - 1, members // group, members), jnp.float32),
            pltpu.VMEM((members // group, members), jnp.float32),
            pltpu.VMEM((n_z - 1, members // group, members), jnp.float32),
            pltpu.VMEM((members, members), jnp.float32),
            pltpu.SemaphoreType.DMA((2, count)),
            pltpu.SemaphoreType.DMA((2, count)),
            pltpu.SemaphoreType.DMA((others,)),
            pltpu.SemaphoreType.DMA((others,)),
        ],
        compiler_params=pltpu.CompilerParams(collective_id=0, has_side_effects=True),
        name="combine",
    )(terms, values, errors)


def three_parts(x):
    first = x.astype(jnp.bfloat16)
    rest = x - first.astype(jnp.float32)
    second = rest.astype(jnp.bfloat16)
    third = (rest - second.astype(jnp.float32)).astype(jnp.bfloat16)
    return first, second, third


def inverse_factor(work):
    size = work.shape[0]
    step = 8
    lane = lax.broadcasted_iota(jnp.int32, (step, LANES), 1)
    sub = lax.broadcasted_iota(jnp.int32, (step, LANES), 0)
    row_of = lax.broadcasted_iota(jnp.int32, (size, 1), 0)

    def panel(at, carry):
        start = pl.multiple_of(at * step, step)
        left = work[pl.ds(start, step), :LANES]
        right = work[pl.ds(start, step), LANES:]
        cols = [
            jnp.broadcast_to(jnp.sum(jnp.where(lane == start + k, left, 0.0), axis=1, keepdims=True), (step, LANES))
            for k in range(step)
        ]
        for k in range(step):
            scale = lax.rsqrt(jnp.broadcast_to(cols[k][k:k + 1, :], (step, LANES)))
            factor = cols[k] * scale
            below = sub > k

            def eliminate(x):
                row = jnp.broadcast_to(x[k:k + 1, :], (step, LANES)) * scale
                return jnp.where(below, x - factor * row, jnp.where(sub == k, row, x))

            left = eliminate(left)
            right = eliminate(right)
            for m in range(k + 1, step):
                cols[m] = eliminate(cols[m])
        work[pl.ds(start, step), :LANES] = left
        work[pl.ds(start, step), LANES:] = right
        first, second, third = three_parts(left)
        wide = jnp.concatenate([left, right], axis=1)
        one, two, three = three_parts(wide)
        lhs = jnp.concatenate([first, first, second, second, first, third], axis=0)
        rhs = jnp.concatenate([one, two, one, two, three, one], axis=0)
        change = lax.dot_general(lhs, rhs, (((0,), (0,)), ((), ())), preferred_element_type=jnp.float32)
        work[...] = jnp.where(row_of >= start + step, work[...] - change, work[...])
        return carry

    lax.fori_loop(0, size // step, panel, 0)


def dot_exact(a, b, dims):
    return lax.dot_general(a, b, (dims, ((), ())), precision=HIGHEST, preferred_element_type=jnp.float32)


def analyse_kernel(prior, sums, members_hbm, out_ref, piece, first, second, factor, sem):
    rows, members = piece.shape
    load = pltpu.make_async_copy(members_hbm.at[pl.ds(lax.axis_index("obs") * rows, rows)], piece, sem)
    load.start()
    row_at = lax.broadcasted_iota(jnp.int32, (LANES, LANES), 0)
    col_at = lax.broadcasted_iota(jnp.int32, (LANES, LANES), 1)
    eye = jnp.where(row_at == col_at, 1.0, 0.0).astype(jnp.float32)
    first[:, :LANES] = sums[:LANES, :LANES] + prior * eye
    first[:, LANES:] = eye
    inverse_factor(first)
    upper = first[:, LANES:]
    across = dot_exact(sums[LANES:, :LANES], upper, ((1,), (1,)))
    second[:, :LANES] = sums[LANES:, LANES:] + prior * eye - dot_exact(across, across, ((1,), (1,)))
    second[:, LANES:] = eye
    inverse_factor(second)
    lower = second[:, LANES:]
    factor[:LANES, :LANES] = upper
    factor[:LANES, LANES:] = jnp.zeros_like(eye)
    factor[LANES:, LANES:] = lower
    factor[LANES:, :LANES] = -dot_exact(lower, dot_exact(across, upper, ((1,), (0,))), ((1,), (0,)))
    inverse = factor[...]
    moved = jnp.concatenate([sums[0:1, LANES:], sums[1:2, LANES:]], axis=1)
    halfway = jnp.sum(inverse * moved, axis=1, keepdims=True)
    mean_weight = jnp.sum(inverse * halfway, axis=0, keepdims=True)
    transform = (math.sqrt(prior) * inverse + mean_weight).astype(jnp.bfloat16)
    load.wait()
    widened = piece[...].astype(jnp.float32)
    state_mean = jnp.mean(widened, axis=1, keepdims=True)
    anomalies = (widened - state_mean).astype(jnp.bfloat16)
    change = lax.dot_general(anomalies, transform, (((1,), (1,)), ((), ())), preferred_element_type=jnp.float32)
    out_ref[...] = (state_mean + change).astype(jnp.bfloat16)


def analyse(sums, members, n_obs):
    slab_rows, width = members.shape
    rows = slab_rows // n_obs
    return pl.pallas_call(
        functools.partial(analyse_kernel, float(width - 1)),
        out_shape=jax.ShapeDtypeStruct((rows, width), jnp.bfloat16),
        in_specs=[VMEM, ANY],
        out_specs=VMEM,
        scratch_shapes=[
            pltpu.VMEM((rows, width), jnp.bfloat16),
            pltpu.VMEM((LANES, 2 * LANES), jnp.float32),
            pltpu.VMEM((LANES, 2 * LANES), jnp.float32),
            pltpu.VMEM((width, width), jnp.float32),
            pltpu.SemaphoreType.DMA,
        ],
        name="analyse",
    )(sums, members)


def on_device(n_obs, n_state, ensemble, obs_values, obs_error, h_blocks, block_rows, block_cols, block_count):
    members = ensemble[0]
    slab_rows, width = members.shape
    size = h_blocks.shape[-1]
    obs_blocks = obs_values.shape[0] // size
    terms = project(
        members.reshape(slab_rows // size, size, width),
        h_blocks[0, 0],
        block_rows[0],
        block_cols[0],
        block_count,
        obs_blocks,
    )
    sums = combine(
        terms,
        obs_values.reshape(obs_blocks, size),
        obs_error.reshape(obs_blocks, size),
        n_obs,
        n_state,
        obs_blocks,
    )
    return analyse(sums, members, n_obs)[None]


def solution(mesh):
    placed = (
        P("state", None, None),
        P("obs"),
        P("obs"),
        P("obs", "state", None, None, None),
        P("obs", "state", None),
        P("obs", "state", None),
        P("obs", "state"),
    )
    return jax.shard_map(
        functools.partial(on_device, mesh.shape["obs"], mesh.shape["state"]),
        mesh=mesh,
        in_specs=placed,
        out_specs=P("state", "obs", None),
        check_vma=False,
    )
```

time: 280 us -> 62.8 us (0.22)
  waiting for transfers between devices: 124 us -> 0 us
  Pallas kernels: 0 us -> 62 us
  other arithmetic: 61.7 us -> 0 us
  blocking collectives: 39.5 us -> 0 us
  matrix products: 26.2 us -> 0 us
  between operations: 14.9 us -> 0.67 us
  local copies, waits for them, and re-layouts: 12.4 us -> 0 us
    psum x1 -> x0, waiting for transfers between devices: 87 us -> none  [on_device(): lax.psum((gram_part, projected_part), ('obs', 'state'))]
    pallas_call x0 -> x3, Pallas kernels: none -> 62 us  [the longest x1 40.3 us: combine(): pl.pallas_call(functools.partial(combine_kernel, n_obs, n_state), out_sha...]
    another operation x10 -> x0, other arithmetic: 54 us -> none  [the longest x6 34 us: on_device(): lower_factor = jnp.linalg.cholesky(gram_sum + (K - 1) * identity)]
    psum x1 -> x0, blocking collectives: 39.5 us -> none  [on_device(): lax.psum((gram_part, projected_part), ('obs', 'state'))]
    reduce_scatter x1 -> x0, waiting for transfers between devices: 37 us -> none  [on_device(): lax.psum_scatter(slab_term, 'state', scatter_dimension=0, tiled=True)]
    dot_general x9 -> x0, matrix products: 23.6 us -> none  [the longest x2 9.29 us: add_group(): jnp.einsum('mb,bik->mik', onehot, upper_part, preferred_element_type=jnp....]
    another operation x18 -> x0, local copies, waits for them, and re-layouts: 4.61 us -> none
    while x5 -> x0, local copies, waits for them, and re-layouts: 4.11 us -> none  [the longest x1 4.1 us: on_device(): lax.fori_loop(0, group_count, add_group, jnp.zeros((obs_blocks, BS, K), j...]
  transfers between devices with their start and end apart: 2 -> 0, of which waited for: 2 -> 0; matrix products, arithmetic and copies ran while one was open for 1% -> 0% of each run, Pallas kernels for 0% -> 0%
where the time goes in v1:
time: 62.8 us; the launch traced here: 62.6 us
  Pallas kernels  62 us (99%)
  between operations  0.67 us (1%)
    pallas_call x1, Pallas kernels, combine(): pl.pallas_call(functools.partial(combine_kernel, n_obs, n_state), out_sha...  40.3 us
    pallas_call x1, Pallas kernels, analyse(): pl.pallas_call(functools.partial(analyse_kernel, float(width - 1)), out_s...  14.7 us
    pallas_call x1, Pallas kernels, project(): pl.pallas_call(functools.partial(project_kernel, groups), out_shape=jax.S...  6.97 us

profile of v1, /device:TPU:0, one launch (start us, length us, event | category | flops | bytes accessed | tf_op | source)
XLA Modules:
  0.0 62.6 jit_solution(6939868044043356349)
XLA Ops:
  0.7 7.0 %project.1.terms = f32[2,17,128,128]{3,2,1,0:T(8,128)} custom-call(s32[1,64]{1,0:T(1,128)} %bitcast.13, s32[1,64]{1,0:T(1,128)} %bitcast.14, s32[1,1]{1,0:T(1,128)S(6)} %copy.8.count_ref, bf16[8,128,256]{2,1,0:T(8,128)(2,1)} %bitcast.9, bf16[64,128,128]{2,1,0:T(8,128)(2,1)} %bitcast.8), custom_call_target="tpu_custom_call" | custom-call | tf_op jit(solution)/shard_map/project/pallas_call | solution.py:57
  7.6 40.3 %combine.1.sums = f32[256,256]{1,0:T(8,128)} custom-call(f32[2,17,128,128]{3,2,1,0:T(8,128)} %project.1.terms, f32[16,128]{1,0:T(8,128)} %bitcast.11, f32[16,128]{1,0:T(8,128)} %bitcast.12), custom_call_target="tpu_custom_call" | custom-call | tf_op jit(solution)/shard_map/combine/pallas_call | solution.py:234
  47.9 14.7 %analyse.1 = bf16[128,256]{1,0:T(8,128)(2,1)} custom-call(f32[256,256]{1,0:T(8,128)} %combine.1.sums, bf16[1024,256]{1,0:T(8,128)(2,1)} %bitcast.10), custom_call_target="tpu_custom_call" | custom-call | tf_op jit(solution)/shard_map/analyse/pallas_call | solution.py:350

commit v2 on v1

--- a/solution.py
+++ b/solution.py
@@ -9,6 +9,8 @@
 from jax.sharding import PartitionSpec as P
 
 LANES = 128
+SUBLANES = 8
+BLOCKS = ((0, 0), (1, 0), (1, 1))
 MESH = pl.DeviceIdType.MESH
 VMEM = pl.BlockSpec(memory_space=pltpu.VMEM)
 SMEM = pl.BlockSpec(memory_space=pltpu.SMEM)
@@ -19,6 +21,7 @@
 def project_kernel(groups, rows_ref, cols_ref, count_ref, members_hbm, blocks_hbm, out_ref, members, blocks, sems):
     slots = blocks.shape[0]
     per = slots // groups
+    together = math.gcd(per, 16)
     spare = out_ref.shape[1] - 1
     load_members = pltpu.make_async_copy(members_hbm, members, sems.at[groups])
     load_members.start()
@@ -34,20 +37,20 @@
         loads[g].wait()
 
         def add_some(step, carry, g=g):
-            base = g * per + step * 4
+            base = g * per + step * together
             products = []
-            for k in range(4):
+            for k in range(together):
                 products.append(
                     jnp.dot(blocks[base + k], members[cols_ref[0, base + k]], preferred_element_type=jnp.float32)
                 )
-            for k in range(4):
+            for k in range(together):
                 slot = base + k
                 row = jnp.where(slot < live, rows_ref[0, slot], spare)
                 out_ref[0, row] += products[k][:, :LANES]
                 out_ref[1, row] += products[k][:, LANES:]
             return carry
 
-        lax.fori_loop(0, per // 4, add_some, 0)
+        lax.fori_loop(0, per // together, add_some, 0)
 
 
 def project(members, blocks, rows, cols, count, obs_blocks):
@@ -56,7 +59,7 @@
     groups = 4
     return pl.pallas_call(
         functools.partial(project_kernel, groups),
-        out_shape=jax.ShapeDtypeStruct((2, obs_blocks + 1, size, width // 2), jnp.float32),
+        out_shape=pltpu.VMEM((2, obs_blocks + 1, size, width // 2), jnp.float32),
         in_specs=[SMEM, SMEM, SMEM, ANY, ANY],
         out_specs=VMEM,
         scratch_shapes=[
@@ -80,11 +83,15 @@
     return plan
 
 
+def half_turn(row):
+    return jnp.concatenate([row[:, LANES // 2:], row[:, :LANES // 2]], axis=1)
+
+
 def columns_of(row):
     return jnp.transpose(jnp.broadcast_to(row, (LANES, LANES)))
 
 
-def combine_kernel(n_obs, n_state, terms, values_ref, errors_ref, out_ref, got0, got1, errs, innov, white, gram, part_in, mine, z_in, full, send, recv, send_b, recv_b):
+def combine_kernel(n_obs, n_state, terms, values_ref, errors_ref, out_ref, got0, got1, errs, innov, gram, part_in, mine, z_in, full, send, recv, send_b, recv_b):
     state = lax.axis_index("state")
     obs = lax.axis_index("obs")
     core = obs % 2
@@ -92,8 +99,8 @@
     n_z = n_obs // 2
     bits = int(math.log2(n_state))
     group = n_state * 2
-    share = white.shape[0]
-    members = white.shape[1]
+    share = errs.shape[0]
+    members = 2 * terms.shape[3]
     per = share // LANES
 
     def flipped(rel):
@@ -152,7 +159,7 @@
             launch(half, 0, plans[half][0][1][index])
     for k in range(per):
         at_rows = pl.ds(k * LANES, LANES)
-        errs[at_rows] = columns_of(errors_ref[pl.ds(state * per + k, 1), :])
+        errs[at_rows] = 1.0 / columns_of(errors_ref[pl.ds(state * per + k, 1), :])
         innov[at_rows] = columns_of(values_ref[pl.ds(state * per + k, 1), :])
     for at in range(bits):
         for index in range(len(plans[0][at][1])):
@@ -169,18 +176,31 @@
     last = [slot_of[half][bits - 1, 0] for half in range(2)]
     low, high = [got[half][last[half]].reshape(share, LANES) for half in range(2)]
     mean = (jnp.sum(low, axis=1, keepdims=True) + jnp.sum(high, axis=1, keepdims=True)) / members
-    white[:, :LANES] = (low - mean) / errs[...]
-    white[:, LANES:] = (high - mean) / errs[...]
-    weight = (innov[...] - mean) / errs[...]
-    whole = white[...]
-    gram[...] = lax.dot_general(
-        whole, whole, (((0,), (0,)), ((), ())), precision=HIGHEST, preferred_element_type=jnp.float32
-    )
-    gram[0:1, LANES:] = jnp.sum(whole[:, :LANES] * weight, axis=0, keepdims=True)
-    gram[1:2, LANES:] = jnp.sum(whole[:, LANES:] * weight, axis=0, keepdims=True)
+    low = (low - mean) * errs[...]
+    high = (high - mean) * errs[...]
+    weight = (innov[...] - mean) * errs[...]
+    sum_low = jnp.sum(low * weight, axis=0, keepdims=True)
+    sum_high = jnp.sum(high * weight, axis=0, keepdims=True)
+    whole = jnp.concatenate([low, high], axis=1)
+    upper = whole.astype(jnp.bfloat16)
+    rest = (whole - upper.astype(jnp.float32)).astype(jnp.bfloat16)
+    turned = jnp.transpose(upper)
+    square = jnp.dot(turned, upper, preferred_element_type=jnp.float32)
+    cross = jnp.dot(turned, rest, preferred_element_type=jnp.float32)
+    tiles = LANES // SUBLANES
+    for k, (i, j) in enumerate(BLOCKS):
+        block_i, block_j = slice(i * LANES, (i + 1) * LANES), slice(j * LANES, (j + 1) * LANES)
+        block = square[block_i, block_j] + (cross[block_i, block_j] + jnp.transpose(cross[block_j, block_i]))
+        gram[k * tiles:(k + 1) * tiles] = block.reshape(tiles, SUBLANES, LANES)
+    lane = lax.broadcasted_iota(jnp.int32, (1, LANES), 1)
+    for k, row in enumerate([sum_low, half_turn(sum_low), sum_high, half_turn(sum_high)]):
+        at = SUBLANES - 4 + k
+        gram[tiles - 1, at:at + 1, :] = jnp.where(lane < LANES // 2, row, gram[tiles - 1, at:at + 1, :])
+    if gram.shape[0] > len(BLOCKS) * tiles:
+        gram[len(BLOCKS) * tiles:] = jnp.zeros_like(gram[len(BLOCKS) * tiles:])
 
     own = state * 2 + core
-    rows = members // group
+    rows = gram.shape[0] // group
 
     def rows_of(index):
         return pl.ds(index * rows, rows)
@@ -201,7 +221,7 @@
     for k, peer in enumerate(peers):
         index = (own + k + 1) % group
         first.append(send_to(gram.at[rows_of(index)], part_in.at[k], k, peer))
-    total = gram[rows_of(own), :]
+    total = gram[rows_of(own)]
     for k, copy in enumerate(first):
         copy.wait_recv()
         total = total + part_in[k]
@@ -212,7 +232,7 @@
     for k, copy in enumerate(second):
         copy.wait_recv()
         total = total + z_in[k]
-    full[rows_of(own), :] = total
+    full[rows_of(own)] = total
     third = []
     for k, peer in enumerate(peers):
         third.append(send_to(full.at[rows_of(own)], full.at[rows_of(own)], group - 1 + n_z - 1 + k, peer))
@@ -230,10 +250,11 @@
     group = 2 * n_state
     n_z = n_obs // 2
     count = n_state - 1
+    tiles = group * pl.cdiv(len(BLOCKS) * LANES // SUBLANES, group)
     others = 2 * (group - 1) + n_z - 1
     return pl.pallas_call(
         functools.partial(combine_kernel, n_obs, n_state),
-        out_shape=jax.ShapeDtypeStruct((members, members), jnp.float32),
+        out_shape=pltpu.VMEM((tiles, SUBLANES, LANES), jnp.float32),
         in_specs=[VMEM] * 3,
         out_specs=VMEM,
         scratch_shapes=[
@@ -241,12 +262,11 @@
             pltpu.VMEM((count, per, size, members // 2), jnp.float32),
             pltpu.VMEM((per * size, LANES), jnp.float32),
             pltpu.VMEM((per * size, LANES), jnp.float32),
-            pltpu.VMEM((per * size, members), jnp.float32),
-            pltpu.VMEM((members, members), jnp.float32),
-            pltpu.VMEM((group - 1, members // group, members), jnp.float32),
-            pltpu.VMEM((members // group, members), jnp.float32),
-            pltpu.VMEM((n_z - 1, members // group, members), jnp.float32),
-            pltpu.VMEM((members, members), jnp.float32),
+            pltpu.VMEM((tiles, SUBLANES, LANES), jnp.float32),
+            pltpu.VMEM((group - 1, tiles // group, SUBLANES, LANES), jnp.float32),
+            pltpu.VMEM((tiles // group, SUBLANES, LANES), jnp.float32),
+            pltpu.VMEM((n_z - 1, tiles // group, SUBLANES, LANES), jnp.float32),
+            pltpu.VMEM((tiles, SUBLANES, LANES), jnp.float32),
             pltpu.SemaphoreType.DMA((2, count)),
             pltpu.SemaphoreType.DMA((2, count)),
             pltpu.SemaphoreType.DMA((others,)),
@@ -254,7 +274,7 @@
         ],
         compiler_params=pltpu.CompilerParams(collective_id=0, has_side_effects=True),
         name="combine",
-    )(terms, values, errors)
+    )(pltpu.with_memory_space_constraint(terms, pltpu.VMEM), values, errors)
 
 
 def three_parts(x):
@@ -267,7 +287,7 @@
 
 def inverse_factor(work):
     size = work.shape[0]
-    step = 8
+    step = 16
     lane = lax.broadcasted_iota(jnp.int32, (step, LANES), 1)
     sub = lax.broadcasted_iota(jnp.int32, (step, LANES), 0)
     row_of = lax.broadcasted_iota(jnp.int32, (size, 1), 0)
@@ -317,13 +337,15 @@
     load.start()
     row_at = lax.broadcasted_iota(jnp.int32, (LANES, LANES), 0)
     col_at = lax.broadcasted_iota(jnp.int32, (LANES, LANES), 1)
+    tiles = LANES // SUBLANES
+    corner, side, other = [sums[k * tiles:(k + 1) * tiles].reshape(LANES, LANES) for k in range(len(BLOCKS))]
     eye = jnp.where(row_at == col_at, 1.0, 0.0).astype(jnp.float32)
-    first[:, :LANES] = sums[:LANES, :LANES] + prior * eye
+    first[:, :LANES] = corner + prior * eye
     first[:, LANES:] = eye
     inverse_factor(first)
     upper = first[:, LANES:]
-    across = dot_exact(sums[LANES:, :LANES], upper, ((1,), (1,)))
-    second[:, :LANES] = sums[LANES:, LANES:] + prior * eye - dot_exact(across, across, ((1,), (1,)))
+    across = dot_exact(side, upper, ((1,), (1,)))
+    second[:, :LANES] = other + prior * eye - dot_exact(across, across, ((1,), (1,)))
     second[:, LANES:] = eye
     inverse_factor(second)
     lower = second[:, LANES:]
@@ -332,7 +354,11 @@
     factor[LANES:, LANES:] = lower
     factor[LANES:, :LANES] = -dot_exact(lower, dot_exact(across, upper, ((1,), (0,))), ((1,), (0,)))
     inverse = factor[...]
-    moved = jnp.concatenate([sums[0:1, LANES:], sums[1:2, LANES:]], axis=1)
+    lane = lax.broadcasted_iota(jnp.int32, (1, LANES), 1)
+    parts = [corner[LANES - 4 + k:LANES - 3 + k, :] for k in range(4)]
+    moved = jnp.concatenate(
+        [jnp.where(lane < LANES // 2, parts[k], half_turn(parts[k + 1])) for k in (0, 2)], axis=1
+    )
     halfway = jnp.sum(inverse * moved, axis=1, keepdims=True)
     mean_weight = jnp.sum(inverse * halfway, axis=0, keepdims=True)
     transform = (math.sqrt(prior) * inverse + mean_weight).astype(jnp.bfloat16)
@@ -360,7 +386,7 @@
             pltpu.SemaphoreType.DMA,
         ],
         name="analyse",
-    )(sums, members)
+    )(pltpu.with_memory_space_constraint(sums, pltpu.VMEM), members)
 
 
 def on_device(n_obs, n_state, ensemble, obs_values, obs_error, h_blocks, block_rows, block_cols, block_count):

time: 62.8 us -> 51.5 us (0.82)
  Pallas kernels: 62 us -> 50.6 us
    pallas_call x1, Pallas kernels: 14.7 us -> 9.53 us  [analyse(): pl.pallas_call(functools.partial(analyse_kernel, float(width - 1)), out_s...]
    pallas_call x1, Pallas kernels: 6.97 us -> 3.66 us  [project(): pl.pallas_call(functools.partial(project_kernel, groups), out_shape=pltpu...]
    pallas_call x1, Pallas kernels: 40.3 us -> 37.4 us  [combine(): pl.pallas_call(functools.partial(combine_kernel, n_obs, n_state), out_sha...]
where the time goes in v2:
time: 51.5 us; the launch traced here: 51.2 us
  Pallas kernels  50.6 us (98%)
  between operations  0.67 us (1%)
    pallas_call x1, Pallas kernels, combine(): pl.pallas_call(functools.partial(combine_kernel, n_obs, n_state), out_sha...  37.4 us
    pallas_call x1, Pallas kernels, analyse(): pl.pallas_call(functools.partial(analyse_kernel, float(width - 1)), out_s...  9.53 us
    pallas_call x1, Pallas kernels, project(): pl.pallas_call(functools.partial(project_kernel, groups), out_shape=pltpu...  3.66 us

profile of v2, /device:TPU:0, one launch (start us, length us, event | category | flops | bytes accessed | tf_op | source)
XLA Modules:
  0.0 51.2 jit_solution(4073470662603317910)
XLA Ops:
  0.7 3.7 %project.1.terms = f32[2,17,128,128]{3,2,1,0:T(8,128)S(1)} custom-call(s32[1,64]{1,0:T(1,128)} %bitcast.13, s32[1,64]{1,0:T(1,128)} %bitcast.14, s32[1,1]{1,0:T(1,128)S(6)} %copy.8.count_ref, bf16[8,128,256]{2,1,0:T(8,128)(2,1)} %bitcast.9, bf16[64,128,128]{2,1,0:T(8,128)(2,1)} %bitcast.8), custom_call_target="tpu_custom_call" | custom-call | tf_op jit(solution)/shard_map/project/pallas_call | solution.py:60
  4.3 37.4 %combine.1.sums = f32[48,8,128]{2,1,0:T(8,128)S(1)} custom-call(f32[2,17,128,128]{3,2,1,0:T(8,128)S(1)} %project.1.terms, f32[16,128]{1,0:T(8,128)} %bitcast.11, f32[16,128]{1,0:T(8,128)} %bitcast.12), custom_call_target="tpu_custom_call" | custom-call | tf_op jit(solution)/shard_map/combine/pallas_call | solution.py:255
  41.7 9.5 %analyse.1 = bf16[128,256]{1,0:T(8,128)(2,1)} custom-call(f32[48,8,128]{2,1,0:T(8,128)S(1)} %combine.1.sums, bf16[1024,256]{1,0:T(8,128)(2,1)} %bitcast.10), custom_call_target="tpu_custom_call" | custom-call | tf_op jit(solution)/shard_map/analyse/pallas_call | solution.py:376

commit v3 on v2

--- a/solution.py
+++ b/solution.py
@@ -18,57 +18,52 @@
 HIGHEST = lax.Precision.HIGHEST
 
 
-def project_kernel(groups, rows_ref, cols_ref, count_ref, members_hbm, blocks_hbm, out_ref, members, blocks, sems):
+def sort_slots(rows_row, live, obs_blocks, out):
+    slots = rows_row.shape[1]
+    at_row = lax.broadcasted_iota(jnp.int32, (1, slots), 1)
+    key_row = jnp.where(at_row < live, rows_row, obs_blocks).astype(jnp.float32)
+    sub = lax.broadcasted_iota(jnp.int32, (slots, slots), 0)
+    lane = lax.broadcasted_iota(jnp.int32, (slots, slots), 1)
+    keys = jnp.broadcast_to(key_row, (slots, slots))
+    key_col = jnp.sum(jnp.where(sub == lane, keys, 0.0), axis=1, keepdims=True)
+    ahead = (keys < key_col) | ((keys == key_col) & (lane < sub))
+    rank = jnp.sum(jnp.where(ahead, 1.0, 0.0), axis=1, keepdims=True)
+    place = lax.broadcasted_iota(jnp.int32, (slots, LANES), 1).astype(jnp.float32)
+    slot = lax.broadcasted_iota(jnp.int32, (slots, LANES), 0).astype(jnp.float32)
+    chosen = rank == place
+    order = jnp.sum(jnp.where(chosen, slot, 0.0), axis=0, keepdims=True)
+    sorted_key = jnp.sum(jnp.where(chosen, key_col, 0.0), axis=0, keepdims=True)
+    smaller = jnp.sum(jnp.where(key_col < sorted_key, 1.0, 0.0), axis=0, keepdims=True)
+    same = jnp.where(smaller == place[0:1], 0.0, 1.0)
+    upto = jnp.sum(jnp.where(key_col <= place, 1.0, 0.0), axis=0, keepdims=True)
+    present = jnp.sum(jnp.where(key_col == place, 1.0, 0.0), axis=0, keepdims=True)
+    last = jnp.maximum(upto - 1.0, 0.0)
+    out[0:1, :] = order.astype(jnp.int32)
+    out[1:2, :] = same.astype(jnp.int32)
+    out[2:3, :] = last.astype(jnp.int32)
+    out[3:4, :] = jnp.minimum(present, 1.0).astype(jnp.int32)
+    out[4:, :] = jnp.zeros_like(out[4:, :])
+
+
+def project_half(half, lists, cols_ref, members, blocks, running, terms):
     slots = blocks.shape[0]
-    per = slots // groups
-    together = math.gcd(per, 16)
-    spare = out_ref.shape[1] - 1
-    load_members = pltpu.make_async_copy(members_hbm, members, sems.at[groups])
-    load_members.start()
-    loads = []
-    for g in range(groups):
-        part = pl.ds(g * per, per)
-        loads.append(pltpu.make_async_copy(blocks_hbm.at[part], blocks.at[part], sems.at[g]))
-        loads[-1].start()
-    out_ref[...] = jnp.zeros_like(out_ref)
-    live = count_ref[0, 0]
-    load_members.wait()
-    for g in range(groups):
-        loads[g].wait()
-
-        def add_some(step, carry, g=g):
-            base = g * per + step * together
-            products = []
-            for k in range(together):
-                products.append(
-                    jnp.dot(blocks[base + k], members[cols_ref[0, base + k]], preferred_element_type=jnp.float32)
-                )
-            for k in range(together):
-                slot = base + k
-                row = jnp.where(slot < live, rows_ref[0, slot], spare)
-                out_ref[0, row] += products[k][:, :LANES]
-                out_ref[1, row] += products[k][:, LANES:]
-            return carry
-
-        lax.fori_loop(0, per // together, add_some, 0)
-
-
-def project(members, blocks, rows, cols, count, obs_blocks):
-    slots, size, unused = blocks.shape
-    width = members.shape[-1]
-    groups = 4
-    return pl.pallas_call(
-        functools.partial(project_kernel, groups),
-        out_shape=pltpu.VMEM((2, obs_blocks + 1, size, width // 2), jnp.float32),
-        in_specs=[SMEM, SMEM, SMEM, ANY, ANY],
-        out_specs=VMEM,
-        scratch_shapes=[
-            pltpu.VMEM(members.shape, members.dtype),
-            pltpu.VMEM(blocks.shape, blocks.dtype),
-            pltpu.SemaphoreType.DMA((groups + 1,)),
-        ],
-        name="project",
-    )(rows, cols, count, members, blocks)
+    together = math.gcd(slots, 16)
+
+    def add_some(step, total):
+        base = step * together
+        products = []
+        for k in range(together):
+            slot = jnp.clip(lists[0, base + k], 0, slots - 1)
+            picked = members[cols_ref[0, slot], :, half * LANES:(half + 1) * LANES]
+            products.append(jnp.dot(blocks[slot], picked, preferred_element_type=jnp.float32))
+        for k in range(together):
+            total = total * lists[1, base + k].astype(jnp.float32) + products[k]
+            running[base + k] = total
+        return total
+
+    lax.fori_loop(0, slots // together, add_some, jnp.zeros(running.shape[1:], jnp.float32))
+    for row in range(terms.shape[1]):
+        terms[half, row] = running[jnp.clip(lists[2, row], 0, slots - 1)] * lists[3, row].astype(jnp.float32)
 
 
 def stage_plan(bits, order):
@@ -91,7 +86,11 @@
     return jnp.transpose(jnp.broadcast_to(row, (LANES, LANES)))
 
 
-def combine_kernel(n_obs, n_state, terms, values_ref, errors_ref, out_ref, got0, got1, errs, innov, gram, part_in, mine, z_in, full, send, recv, send_b, recv_b):
+def combine_kernel(n_obs, n_state, count_ref, cols_ref, rows_ref, members_hbm, blocks_hbm, values_ref, errors_ref, out_ref, members_in, blocks, sorted_in, lists, running, terms, loads, got0, got1, errs, innov, gram, part_in, mine, z_in, full, send, recv, send_b, recv_b):
+    load_members = pltpu.make_async_copy(members_hbm, members_in, loads.at[0])
+    load_blocks = pltpu.make_async_copy(blocks_hbm, blocks, loads.at[1])
+    load_members.start()
+    load_blocks.start()
     state = lax.axis_index("state")
     obs = lax.axis_index("obs")
     core = obs % 2
@@ -119,6 +118,13 @@
     barrier = pltpu.get_barrier_semaphore()
     for peer in peers + z_peers:
         pl.semaphore_signal(barrier, inc=1, device_id=peer, device_id_type=MESH)
+    sort_slots(rows_ref[...], count_ref[0, 0], terms.shape[1], sorted_in)
+    load_lists = pltpu.make_async_copy(sorted_in, lists, loads.at[2])
+    load_lists.start()
+    load_lists.wait()
+    load_members.wait()
+    load_blocks.wait()
+    project_half(0, lists, cols_ref, members_in, blocks, running, terms)
     pl.semaphore_wait(barrier, len(peers) + len(z_peers))
 
     def piece(half, index):
@@ -154,9 +160,11 @@
         copy.start()
         copies[half, at, rel] = copy
 
-    for index in range(len(plans[0][0][1])):
-        for half in range(2):
-            launch(half, 0, plans[half][0][1][index])
+    for half in range(2):
+        if half == 1:
+            project_half(1, lists, cols_ref, members_in, blocks, running, terms)
+        for rel in plans[half][0][1]:
+            launch(half, 0, rel)
     for k in range(per):
         at_rows = pl.ds(k * LANES, LANES)
         errs[at_rows] = 1.0 / columns_of(errors_ref[pl.ds(state * per + k, 1), :])
@@ -243,23 +251,30 @@
         copy.wait_send()
 
 
-def combine(terms, values, errors, n_obs, n_state, obs_blocks):
-    size = terms.shape[2]
-    members = 2 * terms.shape[3]
+def combine(members, blocks, rows, cols, count, values, errors, n_obs, n_state, obs_blocks):
+    slots, size, unused = blocks.shape
+    width = members.shape[-1]
     per = obs_blocks // n_state
     group = 2 * n_state
     n_z = n_obs // 2
-    count = n_state - 1
+    pieces = n_state - 1
     tiles = group * pl.cdiv(len(BLOCKS) * LANES // SUBLANES, group)
     others = 2 * (group - 1) + n_z - 1
     return pl.pallas_call(
         functools.partial(combine_kernel, n_obs, n_state),
         out_shape=pltpu.VMEM((tiles, SUBLANES, LANES), jnp.float32),
-        in_specs=[VMEM] * 3,
+        in_specs=[SMEM, SMEM, VMEM, ANY, ANY, VMEM, VMEM],
         out_specs=VMEM,
         scratch_shapes=[
-            pltpu.VMEM((count, per, size, members // 2), jnp.float32),
-            pltpu.VMEM((count, per, size, members // 2), jnp.float32),
+            pltpu.VMEM(members.shape, members.dtype),
+            pltpu.VMEM(blocks.shape, blocks.dtype),
+            pltpu.VMEM((SUBLANES, LANES), jnp.int32),
+            pltpu.SMEM((SUBLANES, LANES), jnp.int32),
+            pltpu.VMEM((slots, size, width // 2), jnp.float32),
+            pltpu.VMEM((2, obs_blocks, size, width // 2), jnp.float32),
+            pltpu.SemaphoreType.DMA((3,)),
+            pltpu.VMEM((pieces, per, size, width // 2), jnp.float32),
+            pltpu.VMEM((pieces, per, size, width // 2), jnp.float32),
             pltpu.VMEM((per * size, LANES), jnp.float32),
             pltpu.VMEM((per * size, LANES), jnp.float32),
             pltpu.VMEM((tiles, SUBLANES, LANES), jnp.float32),
@@ -267,14 +282,14 @@
             pltpu.VMEM((tiles // group, SUBLANES, LANES), jnp.float32),
             pltpu.VMEM((n_z - 1, tiles // group, SUBLANES, LANES), jnp.float32),
             pltpu.VMEM((tiles, SUBLANES, LANES), jnp.float32),
-            pltpu.SemaphoreType.DMA((2, count)),
-            pltpu.SemaphoreType.DMA((2, count)),
+            pltpu.SemaphoreType.DMA((2, pieces)),
+            pltpu.SemaphoreType.DMA((2, pieces)),
             pltpu.SemaphoreType.DMA((others,)),
             pltpu.SemaphoreType.DMA((others,)),
         ],
         compiler_params=pltpu.CompilerParams(collective_id=0, has_side_effects=True),
         name="combine",
-    )(pltpu.with_memory_space_constraint(terms, pltpu.VMEM), values, errors)
+    )(count, cols, rows, members, blocks, values, errors)
 
 
 def three_parts(x):
@@ -394,16 +409,12 @@
     slab_rows, width = members.shape
     size = h_blocks.shape[-1]
     obs_blocks = obs_values.shape[0] // size
-    terms = project(
+    sums = combine(
         members.reshape(slab_rows // size, size, width),
         h_blocks[0, 0],
         block_rows[0],
         block_cols[0],
         block_count,
-        obs_blocks,
-    )
-    sums = combine(
-        terms,
         obs_values.reshape(obs_blocks, size),
         obs_error.reshape(obs_blocks, size),
         n_obs,

time: 51.5 us -> 50 us (0.971)
  Pallas kernels: 50.6 us -> 49.1 us
    pallas_call x1 -> x0, Pallas kernels: 3.66 us -> none  [project(): pl.pallas_call(functools.partial(project_kernel, groups), out_shape=pltpu...]
    pallas_call x1, Pallas kernels: 37.4 us -> 39.6 us  [combine(): pl.pallas_call(functools.partial(combine_kernel, n_obs, n_state), out_sha...]
where the time goes in v3:
time: 50 us; the launch traced here: 49.8 us
  Pallas kernels  49.1 us (98%)
  between operations  0.66 us (1%)
    pallas_call x1, Pallas kernels, combine(): pl.pallas_call(functools.partial(combine_kernel, n_obs, n_state), out_sha...  39.6 us
    pallas_call x1, Pallas kernels, analyse(): pl.pallas_call(functools.partial(analyse_kernel, float(width - 1)), out_s...  9.53 us

profile of v3, /device:TPU:0, one launch (start us, length us, event | category | flops | bytes accessed | tf_op | source)
XLA Modules:
  0.0 49.8 jit_solution(349623798465157446)
XLA Ops:
  0.7 39.6 %combine.1.sums = f32[48,8,128]{2,1,0:T(8,128)S(1)} custom-call(s32[1,1]{1,0:T(1,128)S(6)} %copy.8.count_ref, s32[1,64]{1,0:T(1,128)} %bitcast.13, s32[1,64]{1,0:T(1,128)} %bitcast.14, bf16[8,128,256]{2,1,0:T(8,128)(2,1)} %bitcast.9, bf16[64,128,128]{2,1,0:T(8,128)(2,1)} %bitcast.8, f32[16,128]{1,0:T(8,128)} %bitcast.11, f32[16,128]{1,0:T(8,128)} %bitcast.12), custom_call_target="tpu_custom_call" | custom-call | tf_op jit(solution)/shard_map/combine/pallas_call | solution.py:263
  40.3 9.5 %analyse.1 = bf16[128,256]{1,0:T(8,128)(2,1)} custom-call(f32[48,8,128]{2,1,0:T(8,128)S(1)} %combine.1.sums, bf16[1024,256]{1,0:T(8,128)(2,1)} %bitcast.10), custom_call_target="tpu_custom_call" | custom-call | tf_op jit(solution)/shard_map/analyse/pallas_call | solution.py:391

commit v4 on v3

--- a/solution.py
+++ b/solution.py
@@ -109,10 +109,9 @@
             total = total + (1 << bit) * ((own + ((rel >> bit) & 1)) % 2)
         return total
 
-    peers = []
-    for shift in range(1, group):
-        index = (state * 2 + core + shift) % group
-        peers.append((z * 2 + index % 2, index // 2))
+    far_first = sorted(range(1, group), key=lambda rel: -bin(rel // 2).count("1"))
+    peer_index = [flipped(rel // 2) * 2 + (core + rel % 2) % 2 for rel in far_first]
+    peers = [(z * 2 + index % 2, index // 2) for index in peer_index]
     z_peers = [(((z + shift) % n_z) * 2 + core, state) for shift in range(1, n_z)]
 
     barrier = pltpu.get_barrier_semaphore()
@@ -227,8 +226,7 @@
 
     first = []
     for k, peer in enumerate(peers):
-        index = (own + k + 1) % group
-        first.append(send_to(gram.at[rows_of(index)], part_in.at[k], k, peer))
+        first.append(send_to(gram.at[rows_of(peer_index[k])], part_in.at[k], k, peer))
     total = gram[rows_of(own)]
     for k, copy in enumerate(first):
         copy.wait_recv()

time: 50 us -> 50 us (level)
  no operation moved by 1% of the time
where the time goes in v4:
time: 50 us; the launch traced here: 49.8 us
  Pallas kernels  49.1 us (98%)
  between operations  0.66 us (1%)
    pallas_call x1, Pallas kernels, combine(): pl.pallas_call(functools.partial(combine_kernel, n_obs, n_state), out_sha...  39.6 us
    pallas_call x1, Pallas kernels, analyse(): pl.pallas_call(functools.partial(analyse_kernel, float(width - 1)), out_s...  9.52 us

profile of v4, /device:TPU:0, one launch (start us, length us, event | category | flops | bytes accessed | tf_op | source)
XLA Modules:
  0.0 49.8 jit_solution(4231442002798497864)
XLA Ops:
  0.7 39.6 %combine.1.sums = f32[48,8,128]{2,1,0:T(8,128)S(1)} custom-call(s32[1,1]{1,0:T(1,128)S(6)} %copy.8.count_ref, s32[1,64]{1,0:T(1,128)} %bitcast.13, s32[1,64]{1,0:T(1,128)} %bitcast.14, bf16[8,128,256]{2,1,0:T(8,128)(2,1)} %bitcast.9, bf16[64,128,128]{2,1,0:T(8,128)(2,1)} %bitcast.8, f32[16,128]{1,0:T(8,128)} %bitcast.11, f32[16,128]{1,0:T(8,128)} %bitcast.12), custom_call_target="tpu_custom_call" | custom-call | tf_op jit(solution)/shard_map/combine/pallas_call | solution.py:261
  40.3 9.5 %analyse.1 = bf16[128,256]{1,0:T(8,128)(2,1)} custom-call(f32[48,8,128]{2,1,0:T(8,128)S(1)} %combine.1.sums, bf16[1024,256]{1,0:T(8,128)(2,1)} %bitcast.10), custom_call_target="tpu_custom_call" | custom-call | tf_op jit(solution)/shard_map/analyse/pallas_call | solution.py:389
